TPU v7x, 512 devices: a whole 4x8x8 slice. The times are simulated.
512 devices in a mesh: seq: 64 (over z, x, core), head: 8 (over y).
Axes of the slice: x: 4, y: 8, z: 8, core: 2. Of those that a mesh axis runs over, the one named last changes fastest.
Arguments:
- query_proj: bfloat16 [65536, 512], P(('seq', 'head')), may hold values from -4 to 4
- key_proj: bfloat16 [65536, 512], P(('seq', 'head')), may hold values from -8 to 8
- value_proj: bfloat16 [65536, 4096], P(('seq', 'head')), may hold values from -6.5 to 6.5
- conv_query: float32 [3, 512], replicated, may hold values from -1 to 1
- conv_key: float32 [3, 512], replicated, may hold values from -1 to 1
- conv_value: float32 [3, 4096], replicated, may hold values from -1 to 1
Outputs:
- mixed_out: bfloat16 [65536, 4096], P(('seq', 'head'))
All inputs are finite; a program needn't handle non-finite values.
Results may differ from a plain program's by a relative error of at most 0.0027.
Values may be sent and summed in bfloat16 or wider, within the bound.
A program may use at most 128 MiB of HBM per device.

v0:
```python
import jax
import jax.numpy as jnp
import numpy as np
from jax import lax
from jax.sharding import PartitionSpec as P

KD = 16
VD = 128
SPAN = 128
KERNEL = 3


def carried_in(part, axis, combine, identity):
    place = lax.axis_index(axis)
    gathered = jax.tree.map(lambda a: lax.all_gather(a, axis), part)
    state = jax.tree.map(lambda a, e: jnp.zeros_like(a) + jnp.asarray(e, a.dtype), part, identity)

    def one(step, state):
        return combine(
            state, jax.tree.map(lambda a: lax.dynamic_index_in_dim(a, step, 0, False), gathered)
        )

    return lax.fori_loop(0, place, one, state)


def passed_along(shard, axis, by):
    size = lax.axis_size(axis)
    pairs = [(i, i + by) for i in range(size) if 0 <= i + by < size]
    return lax.ppermute(shard, axis, pairs)


def features(values):
    scaled = values * KD ** (-0.25)
    first_index, second_index = np.triu_indices(KD, 1)
    cross = scaled[..., first_index] * scaled[..., second_index]
    return jnp.concatenate(
        [jnp.ones_like(scaled[..., :1]), scaled, scaled * scaled * 0.5**0.5, cross], axis=-1
    )


def convolve_rows(row_block, before, tap_rows):
    joined = jnp.concatenate([before, row_block], axis=0).astype(jnp.float32)
    length = row_block.shape[0]
    width = tap_rows.shape[0]
    summed = jnp.zeros((length, row_block.shape[1]), jnp.float32)
    for offset in range(width):
        start = width - 1 - offset
        summed = summed + tap_rows[offset] * joined[start : start + length]
    return summed


def combine_sums(earlier, later):
    return (earlier[0] + later[0], earlier[1] + later[1])


def carried_sums(total_state, total_norm):
    identity = (jnp.zeros_like(total_state), jnp.zeros_like(total_norm))
    return carried_in((total_state, total_norm), "seq", combine_sums, identity)


def state_terms(query_float, state_part, norm_part):
    numer_term = jnp.einsum(
        "nchf,nhfv->nchv",
        query_float,
        state_part,
        precision=lax.Precision.HIGHEST,
        preferred_element_type=jnp.float32,
    )
    denom_term = jnp.einsum(
        "nchf,nhf->nch",
        query_float,
        norm_part,
        precision=lax.Precision.HIGHEST,
        preferred_element_type=jnp.float32,
    )
    return (numer_term, denom_term)


def on_device(query_proj, key_proj, value_proj, conv_query, conv_key, conv_value):
    margin = KERNEL - 1
    query_rows, key_rows, value_rows = (
        lax.all_to_all(query_proj, "head", split_axis=1, concat_axis=0, tiled=True),
        lax.all_to_all(key_proj, "head", split_axis=1, concat_axis=0, tiled=True),
        lax.all_to_all(value_proj, "head", split_axis=1, concat_axis=0, tiled=True),
    )
    group_count = lax.axis_size("head")
    group_index = lax.axis_index("head")
    head_count = query_proj.shape[1] // KD // group_count
    taps_query = lax.dynamic_slice_in_dim(
        conv_query, group_index * head_count * KD, head_count * KD, 1
    )
    taps_key = lax.dynamic_slice_in_dim(conv_key, group_index * head_count * KD, head_count * KD, 1)
    taps_value = lax.dynamic_slice_in_dim(
        conv_value, group_index * head_count * VD, head_count * VD, 1
    )
    before = passed_along(
        (query_rows[-margin:], key_rows[-margin:], value_rows[-margin:]), "seq", 1
    )
    query_conv = convolve_rows(query_rows, before[0], taps_query)
    key_conv = convolve_rows(key_rows, before[1], taps_key)
    value_conv = convolve_rows(value_rows, before[2], taps_value).astype(jnp.bfloat16)
    length = query_conv.shape[0]
    block_count = length // SPAN
    query_feat = features(query_conv.reshape(block_count, SPAN, head_count, KD)).astype(
        jnp.bfloat16
    )
    key_feat = features(key_conv.reshape(block_count, SPAN, head_count, KD)).astype(jnp.bfloat16)
    value_block = value_conv.reshape(block_count, SPAN, head_count, VD)
    causal = jnp.arange(SPAN)[:, None] >= jnp.arange(SPAN)[None, :]
    scores = jnp.einsum("nchf,nmhf->nhcm", query_feat, key_feat, preferred_element_type=jnp.float32)
    scores = jnp.where(causal, scores, jnp.float32(0.0))
    inner_den = jnp.sum(scores, axis=-1).transpose(0, 2, 1)
    inner_num = jnp.einsum(
        "nhcm,nmhv->nchv",
        scores.astype(jnp.bfloat16),
        value_block,
        preferred_element_type=jnp.float32,
    )
    block_state = jnp.einsum(
        "nmhf,nmhv->nhfv", key_feat, value_block, preferred_element_type=jnp.float32
    )
    block_norm = jnp.sum(key_feat.astype(jnp.float32), axis=1)
    prefix_state = jnp.concatenate(
        [jnp.zeros_like(block_state[:1]), jnp.cumsum(block_state, axis=0)[:-1]], axis=0
    )
    prefix_norm = jnp.concatenate(
        [jnp.zeros_like(block_norm[:1]), jnp.cumsum(block_norm, axis=0)[:-1]], axis=0
    )
    total_state = prefix_state[-1] + block_state[-1]
    total_norm = prefix_norm[-1] + block_norm[-1]
    query_float = query_feat.astype(jnp.float32)
    numer_term, denom_term = state_terms(query_float, prefix_state, prefix_norm)
    numerator = inner_num + numer_term
    denominator = inner_den + denom_term
    device_state, device_norm = carried_sums(total_state, total_norm)
    numerator = numerator + jnp.einsum(
        "nchf,hfv->nchv",
        query_float,
        device_state,
        precision=lax.Precision.HIGHEST,
        preferred_element_type=jnp.float32,
    )
    denominator = denominator + jnp.einsum(
        "nchf,hf->nch",
        query_float,
        device_norm,
        precision=lax.Precision.HIGHEST,
        preferred_element_type=jnp.float32,
    )
    result_rows = (
        (numerator / denominator[..., None]).astype(jnp.bfloat16).reshape(length, head_count * VD)
    )
    result_rows = lax.all_to_all(result_rows, "head", split_axis=0, concat_axis=1, tiled=True)
    return result_rows


def solution(mesh):
    in_specs = (
        P(("seq", "head"), None),
        P(("seq", "head"), None),
        P(("seq", "head"), None),
        P(),
        P(),
        P(),
    )
    out_specs = P(("seq", "head"), None)
    return jax.shard_map(
        on_device, mesh=mesh, in_specs=in_specs, out_specs=out_specs, check_vma=False
    )
```

profile of v0, /device:TPU:455, one launch (start us, length us, event | category | flops | bytes accessed | tf_op | source)
XLA Modules:
  0.0 331.2 jit_solution(399916114119146279)
XLA Ops:
  6.5 1.7 copy.72
  8.2 6.8 %all-to-all-start.2 = ((bf16[128,8,64]{0,2,1:T(8,128)(2,1)}), bf16[128,8,64]{0,2,1:T(8,128)(2,1)S(1)}, u32[]{:S(2)}, u32[]{:S(2)}) async-start(bf16[128,8,64]{0,2,1:T(8,128)(2,1)} %bitcast.15), calls=%async_computation.2 | async-start | bytes 262144 | tf_op jit(solution)/shard_map/all_to_all | solution.py:83
  15.0 2.3 copy.62
  17.3 5.5 %all-to-all-done.2 = bf16[128,8,64]{0,2,1:T(8,128)(2,1)S(1)} async-done(((bf16[128,8,64]{0,2,1:T(8,128)(2,1)}), bf16[128,8,64]{0,2,1:T(8,128)(2,1)S(1)}, u32[]{:S(2)}, u32[]{:S(2)}) %all-to-all-start.2) | async-done | bytes 131104 | tf_op jit(solution)/shard_map/all_to_all | solution.py:83
  22.8 3.6 %all-to-all-start = ((bf16[128,8,512]{0,2,1:T(8,128)(2,1)}), bf16[128,8,512]{0,2,1:T(8,128)(2,1)S(1)}, u32[]{:S(2)}, u32[]{:S(2)}) async-start(bf16[128,8,512]{0,2,1:T(8,128)(2,1)} %bitcast.3), calls=%async_computation | async-start | bytes 2097152 | tf_op jit(solution)/shard_map/all_to_all | solution.py:84
  28.2 1.3 collective-permute-start.2
  29.5 3.5 %collective-permute-done.2 = bf16[2,64]{0,1:T(8,128)(2,1)S(1)} collective-permute-done((bf16[2,64]{0,1:T(8,128)(2,1)S(1)}, bf16[2,64]{0,1:T(8,128)(2,1)S(1)}, u32[]{:S(2)}, u32[]{:S(2)}) %collective-permute-start.2) | collective-permute-done | bytes 288 | tf_op jit(solution)/shard_map/ppermute | solution.py:29
  34.3 2.1 gather_fusion.3
  36.4 4.7 %fusion.16 = bf16[8,128,4,120]{1,3,2,0:T(8,128)(2,1)} fusion(f32[120,8,128,4]{2,1,3,0:T(8,128)} %gather_fusion.3, f32[120,8,128,4]{2,1,3,0:T(8,128)S(1)} %gather_fusion.2), kind=kLoop, calls=%fused_computation.35 | loop fusion | flops 983040 | bytes 4915200 | tf_op jit(solution)/shard_map/convert.3
  41.1 14.3 %all-to-all-done = bf16[128,8,512]{0,2,1:T(8,128)(2,1)S(1)} async-done(((bf16[128,8,512]{0,2,1:T(8,128)(2,1)}), bf16[128,8,512]{0,2,1:T(8,128)(2,1)S(1)}, u32[]{:S(2)}, u32[]{:S(2)}) %all-to-all-start) | async-done | bytes 1048608 | tf_op jit(solution)/shard_map/all_to_all | solution.py:84
  55.9 1.3 collective-permute-start
  57.4 1.7 collective-permute-done
  62.0 2.3 fusion.34
  66.1 3.4 %all-to-all-start.1 = ((bf16[128,8,64]{0,2,1:T(8,128)(2,1)}), bf16[128,8,64]{0,2,1:T(8,128)(2,1)S(1)}, u32[]{:S(2)}, u32[]{:S(2)}) async-start(bf16[128,8,64]{0,2,1:T(8,128)(2,1)} %bitcast.9), calls=%async_computation.1 | async-start | bytes 262144 | tf_op jit(solution)/shard_map/all_to_all | solution.py:82
  69.5 7.9 %all-to-all-done.1 = bf16[128,8,64]{0,2,1:T(8,128)(2,1)S(1)} async-done(((bf16[128,8,64]{0,2,1:T(8,128)(2,1)}), bf16[128,8,64]{0,2,1:T(8,128)(2,1)S(1)}, u32[]{:S(2)}, u32[]{:S(2)}) %all-to-all-start.1) | async-done | bytes 131104 | tf_op jit(solution)/shard_map/all_to_all | solution.py:82
  77.5 1.3 collective-permute-start.1
  78.8 4.7 %collective-permute-done.1 = bf16[2,64]{0,1:T(8,128)(2,1)S(1)} collective-permute-done((bf16[2,64]{0,1:T(8,128)(2,1)S(1)}, bf16[2,64]{0,1:T(8,128)(2,1)S(1)}, u32[]{:S(2)}, u32[]{:S(2)}) %collective-permute-start.1) | collective-permute-done | bytes 288 | tf_op jit(solution)/shard_map/ppermute | solution.py:29
  83.9 2.1 gather_fusion
  86.0 2.1 gather_fusion.1
  88.2 2.6 convert_reduce_fusion
  90.8 51.5 %all_gather.9 = f32[64,4,153]{2,1,0:T(4,128)} all-gather(f32[1,4,153]{2,1,0:T(4,128)S(1)} %slice_add_fusion.1), channel_id=1, replica_groups=mesh['seq'=64,'head'=8] {'seq'}, dimensions={0}, use_global_device_ids=true | all-gather | bytes 159120 | tf_op jit(solution)/shard_map/all_gather | solution.py:15
  142.4 3.7 %fusion.15 = bf16[8,128,4,120]{1,3,2,0:T(8,128)(2,1)S(1)} fusion(f32[120,8,128,4]{2,1,3,0:T(8,128)} %gather_fusion.1, f32[120,8,128,4]{2,1,3,0:T(8,128)S(1)} %copy-done.2), kind=kLoop, calls=%fused_computation.34 | loop fusion | flops 983040 | bytes 4915200 | tf_op jit(solution)/shard_map/convert.7
  146.7 1.1 fusion.29
  147.9 1.1 select_reduce_fusion
  149.4 1.9 fusion.12
  151.3 4.7 %fusion.1 = f32[8,4,128,128]{3,2,1,0:T(8,128)} fusion(bf16[8,128,4,153]{1,3,2,0:T(8,128)(2,1)S(1)} %pad_maximum_fusion, f32[8,4,153,128]{3,2,1,0:T(8,128)S(1)} %fusion.34), kind=kOutput, calls=%fused_computation.9 | convolution fusion | flops 842268672 | bytes 5701632 | tf_op jit(solution)/shard_map/nchf,nhfv->nchv/dot_general | solution.py:62
  156.0 16.8 %all-gather.2.cloned.1.call-done = f32[64,4,153,128]{3,1,2,0:T(4,128)} async-done(((f32[1,4,153,128]{3,1,2,0:T(4,128)}), f32[64,4,153,128]{3,1,2,0:T(4,128)}) %all-gather.2.cloned.1.call-update) | async-done | bytes 20054032 | tf_op jit(solution)/shard_map/all_gather | solution.py:15
  172.8 111.9 %while.12 = (s32[]{:T(128)}, f32[4,153,128]{2,1,0:T(8,128)S(1)}, f32[4,153]{1,0:T(4,128)S(1)}, s32[]{:T(128)}, f32[64,4,153,128]{3,1,2,0:T(4,128)}, /*index=5*/f...) while((s32[]{:T(128)}, f32[4,153,128]{2,1,0:T(8,128)S(1)}, f32[4,153]{1,0:T(4,128)S(1)}, s32[]{:T(128)}, ...), condition=%wide.region_4.5_spmd, body=%wide.region_3.4_spmd.sunk | while | flops 78953 | bytes 1574199 | solution.py:23
  172.8 1.1 constant_dynamic-slice_fusion.5
  174.7 1.0 constant_dynamic-slice_fusion.5
  176.5 1.0 constant_dynamic-slice_fusion.5
  178.3 1.0 constant_dynamic-slice_fusion.5
  180.1 1.0 constant_dynamic-slice_fusion.5
  181.8 1.0 constant_dynamic-slice_fusion.5
  183.6 1.0 constant_dynamic-slice_fusion.5
  185.4 1.0 constant_dynamic-slice_fusion.5
  187.2 1.0 constant_dynamic-slice_fusion.5
  188.9 1.0 constant_dynamic-slice_fusion.5
  190.7 1.0 constant_dynamic-slice_fusion.5
  192.5 1.0 constant_dynamic-slice_fusion.5
  194.2 1.0 constant_dynamic-slice_fusion.5
  196.0 1.0 constant_dynamic-slice_fusion.5
  197.8 1.0 constant_dynamic-slice_fusion.5
  227.9 1.0 constant_dynamic-slice_fusion.5
  252.7 1.0 constant_dynamic-slice_fusion.5
  285.3 3.5 %fusion.7 = bf16[8,128,4,128]{1,3,2,0:T(8,128)(2,1)S(1)} fusion(f32[8,4,128,128]{3,2,1,0:T(8,128)} %fusion.12, f32[8,4,128,128]{3,2,1,0:T(8,128)} %fusion.1, bf16[8,128,4,153]{1,3,2,0:T(8,128)(2,1)S(1)} %copy-done.1, f32[8,128,4]{1,2,0:T(4,128)S(1)} %bitcast_add_fusion.2, f32[4,153,128]{2,1,0:T(8,128)S(1)} %get-tuple-element.39), kind=kOutput, calls=%fused_computation.19 | convolution fusion | flops 964689920 | bytes 6825984 | tf_op jit(solution)/shard_map/nchf,hfv->nchv/dot_general | solution.py:136
  288.8 34.3 %all_to_all.76 = bf16[8,128,512]{1,2,0:T(8,128)(2,1)S(1)} all-to-all(bf16[8,128,512]{1,2,0:T(8,128)(2,1)S(1)} %bitcast.103), channel_id=1, replica_groups=mesh['seq'=64,'head'=8] {'head'}, dimensions={0} | all-to-all | bytes 2097152 | tf_op jit(solution)/shard_map/all_to_all | solution.py:153
  323.1 1.3 copy.94
  (235 shorter events, 104.8 us)
Async XLA Ops:
  8.2 14.6 %all-to-all-start.2 = ((bf16[128,8,64]{0,2,1:T(8,128)(2,1)}), bf16[128,8,64]{0,2,1:T(8,128)(2,1)S(1)}, u32[]{:S(2)}, u32[]{:S(2)}) async-start(bf16[128,8,64]{0,2,1:T(8,128)(2,1)} %bitcast.15), calls=%async_computation.2 | async-start | bytes 262144 | tf_op jit(solution)/shard_map/all_to_all | solution.py:83
  15.0 11.4 %copy-start.9 = (s32[120]{0:T(128)S(1)}, s32[120]{0:T(128)}, u32[]{:S(2)}) copy-start(s32[120]{0:T(128)} %constant.72) | copy-start | bytes 1444
  15.0 14.5 %copy-start.8 = (s32[120]{0:T(128)S(1)}, s32[120]{0:T(128)}, u32[]{:S(2)}) copy-start(s32[120]{0:T(128)} %constant.73) | copy-start | bytes 1444
  22.8 32.6 %all-to-all-start = ((bf16[128,8,512]{0,2,1:T(8,128)(2,1)}), bf16[128,8,512]{0,2,1:T(8,128)(2,1)S(1)}, u32[]{:S(2)}, u32[]{:S(2)}) async-start(bf16[128,8,512]{0,2,1:T(8,128)(2,1)} %bitcast.3), calls=%async_computation | async-start | bytes 2097152 | tf_op jit(solution)/shard_map/all_to_all | solution.py:84
  26.4 146.4 %all-gather.2.cloned.1.call-start = ((), (), s32[]{:S(2)}) async-start(), calls=%async_computation.4 | async-start | bytes 20367360 | tf_op jit(solution)/shard_map/all_gather | solution.py:15
  28.2 4.8 %collective-permute-start.2 = (bf16[2,64]{0,1:T(8,128)(2,1)S(1)}, bf16[2,64]{0,1:T(8,128)(2,1)S(1)}, u32[]{:S(2)}, u32[]{:S(2)}) collective-permute-start(bf16[2,64]{0,1:T(8,128)(2,1)S(1)} %slice.126), channel_id=1, source_target_pairs={{0,8},{8,16},{16,24},{24,32},{32,40},{40,48},{48,56},{56,64},{64,7... | collective-permute-start | bytes 776 | tf_op jit(solution)/shard_map/ppermute | solution.py:29
  55.9 3.1 collective-permute-start
  60.0 1.3 copy-start.5
  60.3 1.0 copy-start.3
  62.0 3.3 %copy-start.7 = (bf16[128,512]{1,0:T(8,128)(2,1)S(1)}, bf16[128,512]{1,0:T(8,128)(2,1)}, u32[]{:S(2)}) copy-start(bf16[128,512]{1,0:T(8,128)(2,1)} %param.16) | copy-start | bytes 393220
  66.1 11.3 %all-to-all-start.1 = ((bf16[128,8,64]{0,2,1:T(8,128)(2,1)}), bf16[128,8,64]{0,2,1:T(8,128)(2,1)S(1)}, u32[]{:S(2)}, u32[]{:S(2)}) async-start(bf16[128,8,64]{0,2,1:T(8,128)(2,1)} %bitcast.9), calls=%async_computation.1 | async-start | bytes 262144 | tf_op jit(solution)/shard_map/all_to_all | solution.py:82
  77.5 6.0 %collective-permute-start.1 = (bf16[2,64]{0,1:T(8,128)(2,1)S(1)}, bf16[2,64]{0,1:T(8,128)(2,1)S(1)}, u32[]{:S(2)}, u32[]{:S(2)}) collective-permute-start(bf16[2,64]{0,1:T(8,128)(2,1)S(1)} %slice.122), channel_id=1, source_target_pairs={{0,8},{8,16},{16,24},{24,32},{32,40},{40,48},{48,56},{56,64},{64,7... | collective-permute-start | bytes 776 | tf_op jit(solution)/shard_map/ppermute | solution.py:29
  88.1 54.3 %copy-start.2 = (f32[120,8,128,4]{2,1,3,0:T(8,128)S(1)}, f32[120,8,128,4]{2,1,3,0:T(8,128)}, u32[]{:S(2)}) copy-start(f32[120,8,128,4]{2,1,3,0:T(8,128)} %gather_fusion) | copy-start | bytes 5898244
  146.1 1.7 copy-start.6
  146.7 4.6 %copy-start = (bf16[8,128,4,153]{1,3,2,0:T(8,128)(2,1)}, bf16[8,128,4,153]{1,3,2,0:T(8,128)(2,1)S(1)}, u32[]{:S(2)}) copy-start(bf16[8,128,4,153]{1,3,2,0:T(8,128)(2,1)S(1)} %pad_maximum_fusion) | copy-start | bytes 3760132
  147.9 1.5 copy-start.4
  172.8 111.9 %copy-start.1 = (bf16[8,128,4,153]{1,3,2,0:T(8,128)(2,1)S(1)}, bf16[8,128,4,153]{1,3,2,0:T(8,128)(2,1)}, u32[]{:S(2)}) copy-start(bf16[8,128,4,153]{1,3,2,0:T(8,128)(2,1)} %copy-done) | copy-start | bytes 3760132
Sparse Core Ops, SparseCore 0:
  65.5 107.2 all-gather.1
where the time goes:
time: 336 us; the launch traced here: 331 us
  blocking collectives  85.8 us (26%)
  local copies, waits for them, and re-layouts  80.8 us (24%)
  other arithmetic  64.5 us (19%)
  waiting for transfers between devices  54.4 us (16%)
  starting transfers between devices  17.6 us (5%)
  between operations  13.8 us (4%)
  matrix products  13.6 us (4%)
    dynamic_slice x63, local copies, waits for them, and re-layouts, one(): lax.dynamic_index_in_dim(a, step, 0, False)  62.4 us
    all_gather x1, blocking collectives, carried_in(): gathered = jax.tree.map(lambda a: lax.all_gather(a, axis), part)  51.5 us
    add x126, other arithmetic, combine_sums(): return (earlier[0] + later[0], earlier[1] + later[1])  48.7 us
    all_to_all x1, blocking collectives, on_device(): lax.all_to_all(result_rows, 'head', split_axis=0, concat_axis=1, tiled=True)  34.3 us
    all_gather x1, waiting for transfers between devices, carried_in(): gathered = jax.tree.map(lambda a: lax.all_gather(a, axis), part)  16.8 us
    all_to_all x1, waiting for transfers between devices, on_device(): lax.all_to_all(value_proj, 'head', split_axis=1, concat_axis=0, tiled=True)  14.3 us
    ppermute x3, waiting for transfers between devices, passed_along(): return lax.ppermute(shard, axis, pairs)  9.88 us
    another operation x4, other arithmetic  8.56 us
  transfers between devices with their start and end apart: 7, of which 7 were waited for; matrix products, arithmetic and copies ran while one was open for 10% of the time, Pallas kernels for 0%

commit v1 on v0

--- a/solution.py
+++ b/solution.py
@@ -77,11 +77,21 @@
 
 
 def on_device(query_proj, key_proj, value_proj, conv_query, conv_key, conv_value):
+
+    def recover_paths(my_data):
+        prior = jnp.concatenate(
+            lax.all_to_all(
+                jnp.stack(jnp.split(my_data, lax.axis_size("head"), 1), 0), "head", 0, 0
+            ),
+            0,
+        )
+        return prior
+
     margin = KERNEL - 1
     query_rows, key_rows, value_rows = (
         lax.all_to_all(query_proj, "head", split_axis=1, concat_axis=0, tiled=True),
         lax.all_to_all(key_proj, "head", split_axis=1, concat_axis=0, tiled=True),
-        lax.all_to_all(value_proj, "head", split_axis=1, concat_axis=0, tiled=True),
+        recover_paths(value_proj),
     )
     group_count = lax.axis_size("head")
     group_index = lax.axis_index("head")

time: 336 us -> 348 us (1.036)
  local copies, waits for them, and re-layouts: 80.8 us -> 91.8 us
  waiting for transfers between devices: 54.4 us -> 50.7 us
    unnamed x25 -> x32, local copies, waits for them, and re-layouts: 6.21 us -> 15.1 us
    all_to_all x1, waiting for transfers between devices: 5.48 us -> 0.01 us  [on_device(): lax.all_to_all(key_proj, 'head', split_axis=1, concat_axis=0, tiled=True)]
  transfers between devices with their start and end apart: 7 -> 7, of which waited for: 7 -> 6; matrix products, arithmetic and copies ran while one was open for 10% -> 13% of each run, Pallas kernels for 0% -> 0%
where the time goes in v1:
time: 348 us; the launch traced here: 343 us
  local copies, waits for them, and re-layouts  91.8 us (26%)
  blocking collectives  85.5 us (25%)
  other arithmetic  65.8 us (19%)
  waiting for transfers between devices  50.7 us (15%)
  starting transfers between devices  20.7 us (6%)
  between operations  13.8 us (4%)
  matrix products  13.5 us (4%)
    dynamic_slice x63, local copies, waits for them, and re-layouts, one(): lax.dynamic_index_in_dim(a, step, 0, False)  62.4 us
    all_gather x1, blocking collectives, carried_in(): gathered = jax.tree.map(lambda a: lax.all_gather(a, axis), part)  51.2 us
    add x126, other arithmetic, combine_sums(): return (earlier[0] + later[0], earlier[1] + later[1])  48.7 us
    all_to_all x1, blocking collectives, on_device(): lax.all_to_all(result_rows, 'head', split_axis=0, concat_axis=1, tiled=True)  34.3 us
    all_gather x1, waiting for transfers between devices, carried_in(): gathered = jax.tree.map(lambda a: lax.all_gather(a, axis), part)  17.1 us
    all_to_all x1, waiting for transfers between devices, recover_paths(): lax.all_to_all(jnp.stack(jnp.split(my_data, lax.axis_size('head'), 1), 0)...  16.2 us
    unnamed x32, local copies, waits for them, and re-layouts  15.1 us
    ppermute x3, waiting for transfers between devices, passed_along(): return lax.ppermute(shard, axis, pairs)  9.66 us
  transfers between devices with their start and end apart: 7, of which 6 were waited for; matrix products, arithmetic and copies ran while one was open for 13% of the time, Pallas kernels for 0%

profile of v1, /device:TPU:455, one launch (start us, length us, event | category | flops | bytes accessed | tf_op | source)
XLA Modules:
  0.0 342.6 jit_solution(7009587328763848942)
XLA Ops:
  6.5 1.7 copy.51
  8.2 6.8 %all-to-all-start.2 = ((bf16[128,8,64]{0,2,1:T(8,128)(2,1)}), bf16[128,8,64]{0,2,1:T(8,128)(2,1)S(1)}, u32[]{:S(2)}, u32[]{:S(2)}) async-start(bf16[128,8,64]{0,2,1:T(8,128)(2,1)} %bitcast.21), calls=%async_computation.2 | async-start | bytes 262144 | tf_op jit(solution)/shard_map/all_to_all | solution.py:93
  15.0 1.6 bitcast_dynamic-update-slice_fusion.7
  16.6 1.6 bitcast_dynamic-update-slice_fusion.6
  18.2 1.6 bitcast_dynamic-update-slice_fusion.5
  19.8 1.6 bitcast_dynamic-update-slice_fusion.4
  21.3 1.6 bitcast_dynamic-update-slice_fusion.3
  22.9 1.6 bitcast_dynamic-update-slice_fusion.2
  24.5 1.6 bitcast_dynamic-update-slice_fusion.1
  26.0 1.6 bitcast_dynamic-update-slice_fusion
  27.6 6.6 %all-to-all-start = ((bf16[8,128,512]{2,1,0:T(8,128)(2,1)}), bf16[8,128,512]{2,1,0:T(8,128)(2,1)S(1)}, u32[]{:S(2)}, u32[]{:S(2)}) async-start(bf16[8,128,512]{2,1,0:T(8,128)(2,1)} %bitcast_dynamic-update-slice_fusion), calls=%async_computation | async-start | bytes 2097152 | tf_op jit(solution)/shard_map/all_to_all | solution.py:83
  35.2 1.3 collective-permute-start.2
  37.4 1.9 collective-permute-done.2
  40.5 2.1 gather_fusion.3
  42.6 4.7 %fusion.17 = bf16[8,128,4,120]{1,3,2,0:T(8,128)(2,1)} fusion(f32[120,8,128,4]{2,1,3,0:T(8,128)} %gather_fusion.3, f32[120,8,128,4]{2,1,3,0:T(8,128)S(1)} %gather_fusion.2), kind=kLoop, calls=%fused_computation.36 | loop fusion | flops 983040 | bytes 4915200 | tf_op jit(solution)/shard_map/convert.3
  47.3 16.2 %all-to-all-done = bf16[8,128,512]{2,1,0:T(8,128)(2,1)S(1)} async-done(((bf16[8,128,512]{2,1,0:T(8,128)(2,1)}), bf16[8,128,512]{2,1,0:T(8,128)(2,1)S(1)}, u32[]{:S(2)}, u32[]{:S(2)}) %all-to-all-start) | async-done | bytes 1048608 | tf_op jit(solution)/shard_map/all_to_all | solution.py:83
  64.1 1.3 collective-permute-start
  65.5 1.8 collective-permute-done
  67.9 1.6 fusion.13
  72.2 2.3 fusion.33
  76.3 3.4 all-to-all-start.1
  79.7 7.8 %all-to-all-done.1 = bf16[128,8,64]{0,2,1:T(8,128)(2,1)S(1)} async-done(((bf16[128,8,64]{0,2,1:T(8,128)(2,1)}), bf16[128,8,64]{0,2,1:T(8,128)(2,1)S(1)}, u32[]{:S(2)}, u32[]{:S(2)}) %all-to-all-start.1) | async-done | bytes 131104 | tf_op jit(solution)/shard_map/all_to_all | solution.py:92
  87.6 1.3 collective-permute-start.1
  88.9 6.0 %collective-permute-done.1 = bf16[2,64]{0,1:T(8,128)(2,1)S(1)} collective-permute-done((bf16[2,64]{0,1:T(8,128)(2,1)S(1)}, bf16[2,64]{0,1:T(8,128)(2,1)S(1)}, u32[]{:S(2)}, u32[]{:S(2)}) %collective-permute-start.1) | collective-permute-done | bytes 288 | tf_op jit(solution)/shard_map/ppermute | solution.py:29
  95.3 2.1 gather_fusion
  97.4 2.1 gather_fusion.1
  99.5 2.6 convert_reduce_fusion
  102.2 51.2 %all_gather.9 = f32[64,4,153]{2,1,0:T(4,128)} all-gather(f32[1,4,153]{2,1,0:T(4,128)S(1)} %slice_add_fusion.1), channel_id=1, replica_groups=mesh['seq'=64,'head'=8] {'seq'}, dimensions={0}, use_global_device_ids=true | all-gather | bytes 159120 | tf_op jit(solution)/shard_map/all_gather | solution.py:15
  153.5 3.7 %fusion.16 = bf16[8,128,4,120]{1,3,2,0:T(8,128)(2,1)S(1)} fusion(f32[120,8,128,4]{2,1,3,0:T(8,128)} %gather_fusion.1, f32[120,8,128,4]{2,1,3,0:T(8,128)S(1)} %copy-done.2), kind=kLoop, calls=%fused_computation.35 | loop fusion | flops 983040 | bytes 4915200 | tf_op jit(solution)/shard_map/convert.7
  157.9 1.1 fusion.27
  159.0 1.1 select_reduce_fusion
  160.5 1.9 fusion.12
  162.4 4.7 %fusion.1 = f32[8,4,128,128]{3,2,1,0:T(8,128)} fusion(bf16[8,128,4,153]{1,3,2,0:T(8,128)(2,1)S(1)} %pad_maximum_fusion, f32[8,4,153,128]{3,2,1,0:T(8,128)S(1)} %fusion.33), kind=kOutput, calls=%fused_computation.9 | convolution fusion | flops 842268672 | bytes 5701632 | tf_op jit(solution)/shard_map/nchf,nhfv->nchv/dot_general | solution.py:62
  167.1 17.1 %all-gather.2.cloned.1.call-done = f32[64,4,153,128]{3,1,2,0:T(4,128)} async-done(((f32[1,4,153,128]{3,1,2,0:T(4,128)}), f32[64,4,153,128]{3,1,2,0:T(4,128)}) %all-gather.2.cloned.1.call-update) | async-done | bytes 20054032 | tf_op jit(solution)/shard_map/all_gather | solution.py:15
  184.2 111.9 %while.12 = (s32[]{:T(128)}, f32[4,153,128]{2,1,0:T(8,128)S(1)}, f32[4,153]{1,0:T(4,128)S(1)}, s32[]{:T(128)}, f32[64,4,153,128]{3,1,2,0:T(4,128)}, /*index=5*/f...) while((s32[]{:T(128)}, f32[4,153,128]{2,1,0:T(8,128)S(1)}, f32[4,153]{1,0:T(4,128)S(1)}, s32[]{:T(128)}, ...), condition=%wide.region_4.5_spmd, body=%wide.region_3.4_spmd.sunk | while | flops 78953 | bytes 1574199 | solution.py:23
  184.2 1.1 constant_dynamic-slice_fusion.5
  186.1 1.0 constant_dynamic-slice_fusion.5
  187.9 1.0 constant_dynamic-slice_fusion.5
  189.7 1.0 constant_dynamic-slice_fusion.5
  191.4 1.0 constant_dynamic-slice_fusion.5
  193.2 1.0 constant_dynamic-slice_fusion.5
  195.0 1.0 constant_dynamic-slice_fusion.5
  196.7 1.0 constant_dynamic-slice_fusion.5
  203.8 1.0 constant_dynamic-slice_fusion.5
  207.4 1.0 constant_dynamic-slice_fusion.5
  296.7 3.5 %fusion.7 = bf16[8,128,4,128]{1,3,2,0:T(8,128)(2,1)S(1)} fusion(f32[8,4,128,128]{3,2,1,0:T(8,128)} %fusion.12, f32[8,4,128,128]{3,2,1,0:T(8,128)} %fusion.1, bf16[8,128,4,153]{1,3,2,0:T(8,128)(2,1)S(1)} %copy-done.1, f32[8,128,4]{1,2,0:T(4,128)S(1)} %bitcast_add_fusion.2, f32[4,153,128]{2,1,0:T(8,128)S(1)} %get-tuple-element.39), kind=kOutput, calls=%fused_computation.19 | convolution fusion | flops 964689920 | bytes 6825984 | tf_op jit(solution)/shard_map/nchf,hfv->nchv/dot_general | solution.py:146
  300.2 34.3 %all_to_all.62 = bf16[8,128,512]{1,2,0:T(8,128)(2,1)S(1)} all-to-all(bf16[8,128,512]{1,2,0:T(8,128)(2,1)S(1)} %bitcast.124), channel_id=1, replica_groups=mesh['seq'=64,'head'=8] {'head'}, dimensions={0} | all-to-all | bytes 2097152 | tf_op jit(solution)/shard_map/all_to_all | solution.py:163
  334.5 1.3 copy.70
  (242 shorter events, 112.1 us)
Async XLA Ops:
  8.2 19.4 %all-to-all-start.2 = ((bf16[128,8,64]{0,2,1:T(8,128)(2,1)}), bf16[128,8,64]{0,2,1:T(8,128)(2,1)S(1)}, u32[]{:S(2)}, u32[]{:S(2)}) async-start(bf16[128,8,64]{0,2,1:T(8,128)(2,1)} %bitcast.21), calls=%async_computation.2 | async-start | bytes 262144 | tf_op jit(solution)/shard_map/all_to_all | solution.py:93
  15.0 20.0 %copy-start.8 = (s32[120]{0:T(128)S(1)}, s32[120]{0:T(128)}, u32[]{:S(2)}) copy-start(s32[120]{0:T(128)} %constant.72) | copy-start | bytes 1444
  15.0 20.0 %copy-start.9 = (s32[120]{0:T(128)S(1)}, s32[120]{0:T(128)}, u32[]{:S(2)}) copy-start(s32[120]{0:T(128)} %constant.73) | copy-start | bytes 1444
  27.6 35.8 %all-to-all-start = ((bf16[8,128,512]{2,1,0:T(8,128)(2,1)}), bf16[8,128,512]{2,1,0:T(8,128)(2,1)S(1)}, u32[]{:S(2)}, u32[]{:S(2)}) async-start(bf16[8,128,512]{2,1,0:T(8,128)(2,1)} %bitcast_dynamic-update-slice_fusion), calls=%async_computation | async-start | bytes 2097152 | tf_op jit(solution)/shard_map/all_to_all | solution.py:83
  34.2 149.9 %all-gather.2.cloned.1.call-start = ((), (), s32[]{:S(2)}) async-start(), calls=%async_computation.4 | async-start | bytes 20367360 | tf_op jit(solution)/shard_map/all_gather | solution.py:15
  35.2 4.1 %collective-permute-start.2 = (bf16[2,64]{0,1:T(8,128)(2,1)S(1)}, bf16[2,64]{0,1:T(8,128)(2,1)S(1)}, u32[]{:S(2)}, u32[]{:S(2)}) collective-permute-start(bf16[2,64]{0,1:T(8,128)(2,1)S(1)} %slice.126), channel_id=1, source_target_pairs={{0,8},{8,16},{16,24},{24,32},{32,40},{40,48},{48,56},{56,64},{64,7... | collective-permute-start | bytes 776 | tf_op jit(solution)/shard_map/ppermute | solution.py:29
  64.1 3.2 collective-permute-start
  69.6 2.1 copy-start.5
  70.7 1.0 copy-start.3
  72.2 3.3 copy-start.7
  76.3 11.2 %all-to-all-start.1 = ((bf16[128,8,64]{0,2,1:T(8,128)(2,1)}), bf16[128,8,64]{0,2,1:T(8,128)(2,1)S(1)}, u32[]{:S(2)}, u32[]{:S(2)}) async-start(bf16[128,8,64]{0,2,1:T(8,128)(2,1)} %bitcast.15), calls=%async_computation.1 | async-start | bytes 262144 | tf_op jit(solution)/shard_map/all_to_all | solution.py:92
  87.6 7.3 %collective-permute-start.1 = (bf16[2,64]{0,1:T(8,128)(2,1)S(1)}, bf16[2,64]{0,1:T(8,128)(2,1)S(1)}, u32[]{:S(2)}, u32[]{:S(2)}) collective-permute-start(bf16[2,64]{0,1:T(8,128)(2,1)S(1)} %slice.122), channel_id=1, source_target_pairs={{0,8},{8,16},{16,24},{24,32},{32,40},{40,48},{48,56},{56,64},{64,7... | collective-permute-start | bytes 776 | tf_op jit(solution)/shard_map/ppermute | solution.py:29
  99.5 54.0 %copy-start.2 = (f32[120,8,128,4]{2,1,3,0:T(8,128)S(1)}, f32[120,8,128,4]{2,1,3,0:T(8,128)}, u32[]{:S(2)}) copy-start(f32[120,8,128,4]{2,1,3,0:T(8,128)} %gather_fusion) | copy-start | bytes 5898244
  157.3 1.7 copy-start.6
  157.9 4.5 %copy-start = (bf16[8,128,4,153]{1,3,2,0:T(8,128)(2,1)}, bf16[8,128,4,153]{1,3,2,0:T(8,128)(2,1)S(1)}, u32[]{:S(2)}) copy-start(bf16[8,128,4,153]{1,3,2,0:T(8,128)(2,1)S(1)} %pad_maximum_fusion) | copy-start | bytes 3760132
  159.0 1.5 copy-start.4
  184.2 111.9 %copy-start.1 = (bf16[8,128,4,153]{1,3,2,0:T(8,128)(2,1)S(1)}, bf16[8,128,4,153]{1,3,2,0:T(8,128)(2,1)}, u32[]{:S(2)}) copy-start(bf16[8,128,4,153]{1,3,2,0:T(8,128)(2,1)} %copy-done) | copy-start | bytes 3760132
Sparse Core Ops, SparseCore 0:
  75.7 108.4 all-gather.1
